TPU v7x, 32 devices: a whole 2x2x4 slice. The times are simulated.
32 devices in a mesh: pair: 2 (over core), vcol: 16 (over z, y, x).
Axes of the slice: x: 2, y: 2, z: 4, core: 2. Of those that a mesh axis runs over, the one named last changes fastest.
Arguments:
- amplitudes: bfloat16 [1280, 4096], P('pair', 'vcol'), may hold values from -6 to 6
- tile_owner: int32 [32], replicated, may hold values from 0 to 31, each once
- integrals: bfloat16 [4096, 4096], P('pair', 'vcol'), may hold values from -0.125 to 0.125
- screening: int32 [20, 32, 32], P('pair'), may hold values 0 or 1
- occ_energy: float32 [1280], P('pair'), may hold values from -1 to -0.2
- virt_energy: float32 [4096], replicated, may hold values from 0.2 to 1
Outputs:
- residual: bfloat16 [1280, 4096], P('pair', 'vcol')
Inputs may be any that keep to these rules, and one draw needn't show every extreme that they name: `tile_owner`: each of the 32 tiles appears exactly once.
All inputs are finite; a program needn't handle non-finite values. No bound on the sum of `screening` on one device may be relied on, other than what follows from the above.
Results may differ from a plain program's by a relative error of at most 0.0036.
Values may be sent and summed in bfloat16 or wider, within the bound.
A program may use at most 64 MiB of HBM per device.

v0:
```python
import jax
import jax.numpy as jnp
from jax import lax
from jax.sharding import PartitionSpec as P

TILE = 128
PBLK = 64
KT_DEV = 2


def one_hot(indices, length):
    return (indices[:, None] == jnp.arange(length, dtype=jnp.int32)[None, :]).astype(jnp.float32)


def gather_rows(panel):
    return lax.all_gather(panel, "pair", axis=0, tiled=True)


def local(amplitudes, tile_owner, integrals, screening, occ_energy, virt_energy):
    pair_local = amplitudes.shape[0]
    tile_count = tile_owner.shape[0]
    width = KT_DEV * TILE
    block_count = pair_local // PBLK
    column = lax.axis_index("vcol")
    first_slot = column * KT_DEV
    owned_tiles = lax.dynamic_slice_in_dim(tile_owner, first_slot, KT_DEV, 0)
    screen_float = screening.astype(jnp.float32)
    natural_tiles = first_slot + jnp.arange(KT_DEV, dtype=jnp.int32)
    panel = gather_rows(integrals)
    picked = jnp.einsum("bct,jt->bcj", screen_float, one_hot(natural_tiles, tile_count))
    marks_slot = jnp.take(picked, tile_owner, axis=1).astype(jnp.bfloat16)
    panel_slot = jnp.take(panel.reshape(tile_count, TILE, width), tile_owner, axis=0)
    piece_in = lax.all_gather(amplitudes, "vcol", axis=1, tiled=True)
    tiles_in = piece_in.shape[1] // TILE
    left_all = piece_in.reshape(block_count, PBLK, tiles_in * TILE)

    def one_block(operands):
        left_rows, marks = operands
        masked = (
            panel_slot.reshape(tiles_in, TILE, KT_DEV, TILE) * marks[:, None, :, None]
        ).reshape(tiles_in * TILE, width)
        return jnp.dot(left_rows, masked, preferred_element_type=jnp.float32)

    summed = lax.map(one_block, (left_all, marks_slot))
    ladder_local = summed.reshape(pair_local, width).astype(jnp.bfloat16)
    piece_in = lax.all_gather(ladder_local, "vcol", axis=1, tiled=True)
    tiles_in = piece_in.shape[1] // TILE
    chooser = one_hot(owned_tiles, tiles_in).astype(jnp.bfloat16)
    shaped = piece_in.reshape(piece_in.shape[0], tiles_in, TILE)
    ladder_owned = jnp.einsum(
        "pmk,jm->pjk", shaped, chooser, preferred_element_type=jnp.float32
    ).reshape(pair_local, width)
    virt_owned = jnp.dot(
        one_hot(owned_tiles, tile_count),
        virt_energy.reshape(tile_count, TILE),
        precision=lax.Precision.HIGHEST,
    ).reshape(width)
    residual = ladder_owned + (virt_owned[None, :] - occ_energy[:, None]) * amplitudes.astype(
        jnp.float32
    )
    return residual.astype(jnp.bfloat16)


def solution(mesh):
    return jax.shard_map(
        local,
        mesh=mesh,
        in_specs=(P("pair", "vcol"), P(), P("pair", "vcol"), P("pair", None, None), P("pair"), P()),
        out_specs=P("pair", "vcol"),
        check_vma=False,
    )
```

profile of v0, /device:TPU:0, one launch (start us, length us, event | category | flops | bytes accessed | tf_op | source)
XLA Modules:
  0.0 258.9 jit_solution(7271926033626075725)
XLA Ops:
  6.5 0.7 all-gather.6.cloned.1.call-update
  7.3 0.7 all-gather.4.cloned.1.call-update
  8.1 1.2 convolution_bitcast_fusion.1
  9.2 0.1 copy.9
  9.4 0.7 compare_select_fusion
  10.1 0.6 gather_fusion
  10.7 0.7 compare_and_fusion
  11.3 0.1 fusion.8
  11.5 10.7 %all-gather.6.cloned.1.call-done = bf16[4096,256]{1,0:T(8,128)(2,1)} async-done(((bf16[2048,256]{1,0:T(8,128)(2,1)}), bf16[4096,256]{1,0:T(8,128)(2,1)}) %all-gather.6.cloned.1.call-update) | async-done | bytes 2097168 | tf_op jit(solution)/shard_map/all_gather | solution.py:16
  22.2 3.7 %gather_fusion.1 = bf16[32,128,256]{2,1,0:T(8,128)(2,1)} fusion(bf16[32,128,256]{2,1,0:T(8,128)(2,1)} %bitcast.60, s32[1024]{0:T(1024)S(1)} %pad_clamp_fusion), kind=kCustom, calls=%fused_computation.1 | custom fusion | bytes 4194432 | tf_op jit(solution)/shard_map/jit(_take)/gather | solution.py:32
  25.9 1.8 broadcast_select_fusion
  27.7 96.8 %all-gather.4.cloned.1.call-done = bf16[640,4096]{1,0:T(8,128)(2,1)} async-done(((bf16[640,256]{1,0:T(8,128)(2,1)}), bf16[640,4096]{1,0:T(8,128)(2,1)}) %all-gather.4.cloned.1.call-update) | async-done | bytes 5242896 | tf_op jit(solution)/shard_map/all_gather | solution.py:33
  124.5 25.2 %while.10 = (s32[]{:T(128)}, bf16[10,64,256]{2,1,0:T(8,128)(2,1)}, bf16[10,64,4096]{2,1,0:T(8,128)(2,1)}, bf16[10,32,2]{1,2,0:T(2,128)(2,1)S(1)}, bf16[32,128,256]{2,1,0:T(8,128)(2,1)S(1)}, /*index=5*/s32[]{:T(128)}) while((s32[]{:T(128)}, bf16[10,64,256]{2,1,0:T(8,128)(2,1)}, bf16[10,64,4096]{2,1,0:T(8,128)(2,1)}, ...), condition=%wide.region_1.2_spmd, body=%wide.region_0.1_spmd.sunk | while | flops 135266304 | bytes 6948553 | solution.py:44
  124.5 0.1 copy.19
  124.7 0.1 broadcast_multiply_fusion.2
  124.9 2.1 fusion.27
  127.0 0.1 copy.19
  127.2 0.1 broadcast_multiply_fusion.2
  127.4 2.1 fusion.27
  129.5 0.1 copy.19
  129.8 0.1 broadcast_multiply_fusion.2
  129.9 2.1 fusion.27
  132.1 0.1 copy.19
  132.3 0.1 broadcast_multiply_fusion.2
  132.4 2.1 fusion.27
  134.6 0.1 copy.19
  134.8 0.1 broadcast_multiply_fusion.2
  135.0 2.1 fusion.27
  137.1 0.1 copy.19
  137.3 0.1 broadcast_multiply_fusion.2
  137.5 2.1 fusion.27
  139.6 0.1 copy.19
  139.8 0.1 broadcast_multiply_fusion.2
  140.0 2.1 fusion.27
  142.1 0.1 copy.19
  142.4 0.1 broadcast_multiply_fusion.2
  142.5 2.1 fusion.27
  144.6 0.1 copy.19
  144.9 0.1 broadcast_multiply_fusion.2
  145.0 2.1 fusion.27
  147.2 0.1 copy.19
  147.4 0.1 broadcast_multiply_fusion.2
  147.5 2.1 fusion.27
  149.8 0.2 convolution_bitcast_fusion.2
  150.0 96.4 %all-gather.8.cloned.1.call-done = bf16[640,4096]{1,0:T(8,128)(2,1)} async-done(((bf16[640,256]{1,0:T(8,128)(2,1)}), bf16[640,4096]{1,0:T(8,128)(2,1)}) %all-gather.8.cloned.1.call-update) | async-done | bytes 5242896 | tf_op jit(solution)/shard_map/all_gather | solution.py:46
  246.4 4.1 %copy.12 = bf16[80,8,32,128]{3,2,1,0:T(8,128)(2,1)S(1)} copy(bf16[80,8,32,128]{3,1,2,0:T(8,128)(2,1)} %bitcast.58) | data formatting | bytes 10485760
  250.6 0.9 fusion.13
  251.5 0.9 fusion.5
  (47 shorter events, 1.5 us)
Async XLA Ops:
  6.5 143.3 %copy-start = (f32[4096]{0:T(1024)S(1)}, f32[4096]{0:T(1024)}, u32[]{:S(2)}) copy-start(f32[4096]{0:T(1024)} %param.13) | copy-start | bytes 49156
  6.5 15.7 %all-gather.6.cloned.1.call-start = ((), (), s32[]{:S(2)}) async-start(), calls=%async_computation.1 | async-start | bytes 3145728 | tf_op jit(solution)/shard_map/all_gather | solution.py:16
  7.3 117.2 %all-gather.4.cloned.1.call-start = ((), (), s32[]{:S(2)}) async-start(), calls=%async_computation | async-start | bytes 5570560 | tf_op jit(solution)/shard_map/all_gather | solution.py:33
  8.0 238.4 %all-gather.8.cloned.1.call-start = ((), (), s32[]{:S(2)}) async-start(), calls=%async_computation.2 | async-start | bytes 5570560 | tf_op jit(solution)/shard_map/all_gather | solution.py:46
  124.5 25.2 %copy-start.3 = (s32[32]{0:T(128)S(1)}, s32[32]{0:T(128)}, u32[]{:S(2)}) copy-start(s32[32]{0:T(128)} %param.9) | copy-start | bytes 388
  250.5 1.0 copy-start.1
  250.5 1.0 copy-start.2
Sparse Core Ops, SparseCore 0:
  8.9 13.2 all-gather.5
  24.9 99.5 all-gather.3
  149.8 96.5 all-gather.7
where the time goes:
time: 260 us; the launch traced here: 259 us
  waiting for transfers between devices  205 us (79%)
  matrix products  23.6 us (9%)
  between operations  13.2 us (5%)
  local copies, waits for them, and re-layouts  10.9 us (4%)
  other arithmetic  5.66 us (2%)
    all_gather x1, waiting for transfers between devices, local(): piece_in = lax.all_gather(amplitudes, 'vcol', axis=1, tiled=True)  96.8 us
    all_gather x1, waiting for transfers between devices, local(): piece_in = lax.all_gather(ladder_local, 'vcol', axis=1, tiled=True)  96.4 us
    dot_general x10, matrix products, one_block(): return jnp.dot(left_rows, masked, preferred_element_type=jnp.float32)  21.4 us
    all_gather x1, waiting for transfers between devices, gather_rows(): return lax.all_gather(panel, 'pair', axis=0, tiled=True)  10.7 us
  transfers between devices with their start and end apart: 3, of which 3 were waited for; matrix products, arithmetic and copies ran while one was open for 4% of the time, Pallas kernels for 0%

commit v1 on v0

--- a/solution.py
+++ b/solution.py
@@ -43,13 +43,13 @@
 
     summed = lax.map(one_block, (left_all, marks_slot))
     ladder_local = summed.reshape(pair_local, width).astype(jnp.bfloat16)
-    piece_in = lax.all_gather(ladder_local, "vcol", axis=1, tiled=True)
-    tiles_in = piece_in.shape[1] // TILE
-    chooser = one_hot(owned_tiles, tiles_in).astype(jnp.bfloat16)
-    shaped = piece_in.reshape(piece_in.shape[0], tiles_in, TILE)
-    ladder_owned = jnp.einsum(
-        "pmk,jm->pjk", shaped, chooser, preferred_element_type=jnp.float32
-    ).reshape(pair_local, width)
+    ranks = tile_count // KT_DEV
+    rows = pair_local // ranks
+    parts = ladder_local.reshape(ranks, rows, KT_DEV, TILE).transpose(0, 2, 1, 3)
+    spread = lax.all_to_all(parts, "vcol", 0, 0, tiled=True).reshape(tile_count, rows, TILE)
+    by_slot = jnp.take(spread, tile_owner, axis=0).reshape(ranks, KT_DEV, rows, TILE)
+    back = lax.all_to_all(by_slot, "vcol", 0, 0, tiled=True)
+    ladder_owned = back.transpose(0, 2, 1, 3).reshape(pair_local, width).astype(jnp.float32)
     virt_owned = jnp.dot(
         one_hot(owned_tiles, tile_count),
         virt_energy.reshape(tile_count, TILE),

time: 260 us -> 185 us (0.71)
  waiting for transfers between devices: 205 us -> 131 us
  starting transfers between devices: 0.08 us -> 7.39 us
  matrix products: 23.6 us -> 16.5 us
    all_gather x1 -> x0, waiting for transfers between devices: 96.4 us -> none  [local(): piece_in = lax.all_gather(ladder_local, 'vcol', axis=1, tiled=True)]
    all_to_all x0 -> x2, waiting for transfers between devices: none -> 21.7 us  [the longest x1 11.2 us: local(): lax.all_to_all(parts, 'vcol', 0, 0, tiled=True)]
    all_to_all x0 -> x2, starting transfers between devices: none -> 7.34 us  [the longest x1 3.8 us: local(): lax.all_to_all(parts, 'vcol', 0, 0, tiled=True)]
    dot_general x10, matrix products: 21.4 us -> 15.1 us  [one_block(): return jnp.dot(left_rows, masked, preferred_element_type=jnp.float32)]
    unnamed x9 -> x8, local copies, waits for them, and re-layouts: 4.23 us -> 0.02 us
  transfers between devices with their start and end apart: 3 -> 4, of which waited for: 3 -> 4; matrix products, arithmetic and copies ran while one was open for 4% -> 5% of each run, Pallas kernels for 0% -> 0%
where the time goes in v1:
time: 185 us; the launch traced here: 184 us
  waiting for transfers between devices  131 us (71%)
  matrix products  16.5 us (9%)
  between operations  13.5 us (7%)
  local copies, waits for them, and re-layouts  8.64 us (5%)
  starting transfers between devices  7.39 us (4%)
  other arithmetic  6.53 us (4%)
    all_gather x1, waiting for transfers between devices, local(): piece_in = lax.all_gather(amplitudes, 'vcol', axis=1, tiled=True)  96.8 us
    dot_general x10, matrix products, one_block(): return jnp.dot(left_rows, masked, preferred_element_type=jnp.float32)  15.1 us
    all_to_all x1, waiting for transfers between devices, local(): lax.all_to_all(parts, 'vcol', 0, 0, tiled=True)  11.2 us
    all_gather x1, waiting for transfers between devices, gather_rows(): return lax.all_gather(panel, 'pair', axis=0, tiled=True)  10.7 us
    all_to_all x1, waiting for transfers between devices, local(): back = lax.all_to_all(by_slot, 'vcol', 0, 0, tiled=True)  10.4 us
    all_to_all x1, starting transfers between devices, local(): lax.all_to_all(parts, 'vcol', 0, 0, tiled=True)  3.8 us
  transfers between devices with their start and end apart: 4, of which 4 were waited for; matrix products, arithmetic and copies ran while one was open for 5% of the time, Pallas kernels for 0%

profile of v1, /device:TPU:0, one launch (start us, length us, event | category | flops | bytes accessed | tf_op | source)
XLA Modules:
  0.0 183.6 jit_solution(1509187314705847250)
XLA Ops:
  6.5 0.7 all-gather.5.cloned.1.call-update
  7.3 0.7 all-gather.3.cloned.1.call-update
  8.0 1.2 convolution_bitcast_fusion.1
  9.2 0.1 copy.12
  9.3 0.7 compare_select_fusion
  10.0 0.6 gather_fusion
  10.6 0.7 compare_and_fusion
  11.3 0.1 fusion.8
  11.5 10.7 %all-gather.5.cloned.1.call-done = bf16[4096,256]{1,0:T(8,128)(2,1)} async-done(((bf16[2048,256]{1,0:T(8,128)(2,1)}), bf16[4096,256]{1,0:T(8,128)(2,1)}) %all-gather.5.cloned.1.call-update) | async-done | bytes 2097168 | tf_op jit(solution)/shard_map/all_gather | solution.py:16
  22.2 3.7 %gather_fusion.1 = bf16[32,128,256]{2,1,0:T(8,128)(2,1)} fusion(bf16[32,128,256]{2,1,0:T(8,128)(2,1)} %bitcast.56, s32[1024]{0:T(1024)S(1)} %pad_clamp_fusion), kind=kCustom, calls=%fused_computation.1 | custom fusion | bytes 4194432 | tf_op jit(solution)/shard_map/jit(_take)/gather | solution.py:32
  25.9 1.8 %broadcast_select_fusion = bf16[32,128,256]{2,1,0:T(8,128)(2,1)S(1)} fusion(bf16[32,128,256]{2,1,0:T(8,128)(2,1)} %gather_fusion.1, pred[32]{0:T(512)(128)(4,1)S(1)} %compare_and_fusion), kind=kLoop, calls=%fused_computation.12 | loop fusion | flops 1048576 | bytes 4194336 | tf_op jit(solution)/shard_map/jit(_take)/select_n | solution.py:32
  27.7 96.8 %all-gather.3.cloned.1.call-done = bf16[640,4096]{1,0:T(8,128)(2,1)} async-done(((bf16[640,256]{1,0:T(8,128)(2,1)}), bf16[640,4096]{1,0:T(8,128)(2,1)}) %all-gather.3.cloned.1.call-update) | async-done | bytes 5242896 | tf_op jit(solution)/shard_map/all_gather | solution.py:33
  124.5 19.2 %while.10 = (s32[]{:T(128)}, bf16[10,64,256]{2,1,0:T(8,128)(2,1)S(1)}, bf16[10,64,4096]{2,1,0:T(8,128)(2,1)}, bf16[10,32,2]{1,2,0:T(2,128)(2,1)S(1)}, bf16[32,128,256]{2,1,0:T(8,128)(2,1)S(1)}, /*index=5*/s32[]{:T(128)}) while((s32[]{:T(128)}, bf16[10,64,256]{2,1,0:T(8,128)(2,1)S(1)}, bf16[10,64,4096]{2,1,0:T(8,128)(2,1)}, ...), condition=%wide.region_1.2_spmd, body=%wide.region_0.1_spmd.sunk | while | flops 135266304 | bytes 6948553 | solution.py:44
  124.5 0.1 copy.23
  124.7 0.1 broadcast_multiply_fusion.2
  124.9 1.5 fusion.24
  126.7 0.1 broadcast_multiply_fusion.2
  126.8 1.5 fusion.24
  128.4 0.1 copy.23
  128.6 0.1 broadcast_multiply_fusion.2
  128.7 1.5 fusion.24
  130.5 0.1 broadcast_multiply_fusion.2
  130.7 1.5 fusion.24
  132.2 0.1 copy.23
  132.4 0.1 broadcast_multiply_fusion.2
  132.6 1.5 fusion.24
  134.4 0.1 broadcast_multiply_fusion.2
  134.5 1.5 fusion.24
  136.1 0.1 copy.23
  136.3 0.1 broadcast_multiply_fusion.2
  136.4 1.5 fusion.24
  138.2 0.1 broadcast_multiply_fusion.2
  138.4 1.5 fusion.24
  139.9 0.1 copy.23
  140.1 0.1 broadcast_multiply_fusion.2
  140.3 1.5 fusion.24
  142.0 0.1 broadcast_multiply_fusion.2
  142.2 1.5 fusion.24
  143.7 0.8 convert_element_type.33
  144.5 3.8 %all-to-all-start = ((bf16[16,2,40,128]{3,1,2,0:T(2,128)(2,1)}), bf16[16,2,40,128]{3,1,2,0:T(2,128)(2,1)S(1)}, u32[]{:S(2)}, u32[]{:S(2)}) async-start(bf16[16,2,40,128]{3,1,2,0:T(2,128)(2,1)} %bitcast.9), calls=%async_computation | async-start | bytes 655360 | tf_op jit(solution)/shard_map/all_to_all | solution.py:49
  148.4 11.2 %all-to-all-done = bf16[16,2,40,128]{3,1,2,0:T(2,128)(2,1)S(1)} async-done(((bf16[16,2,40,128]{3,1,2,0:T(2,128)(2,1)}), bf16[16,2,40,128]{3,1,2,0:T(2,128)(2,1)S(1)}, u32[]{:S(2)}, u32[]{:S(2)}) %all-to-all-start) | async-done | bytes 327712 | tf_op jit(solution)/shard_map/all_to_all | solution.py:49
  159.7 0.6 gather_fusion.2
  160.4 0.8 broadcast_select_fusion.1
  161.2 3.5 %all-to-all-start.1 = ((bf16[16,2,40,128]{3,2,1,0:T(8,128)(2,1)}), bf16[16,2,40,128]{3,2,1,0:T(8,128)(2,1)S(1)}, u32[]{:S(2)}, u32[]{:S(2)}) async-start(bf16[16,2,40,128]{3,2,1,0:T(8,128)(2,1)} %broadcast_select_fusion.1), calls=%async_computation.1 | async-start | bytes 655360 | tf_op jit(solution)/shard_map/all_to_all | solution.py:51
  164.8 0.2 convolution_bitcast_fusion.2
  165.0 10.4 %all-to-all-done.1 = bf16[16,2,40,128]{3,2,1,0:T(8,128)(2,1)S(1)} async-done(((bf16[16,2,40,128]{3,2,1,0:T(8,128)(2,1)}), bf16[16,2,40,128]{3,2,1,0:T(8,128)(2,1)S(1)}, u32[]{:S(2)}, u32[]{:S(2)}) %all-to-all-start.1) | async-done | bytes 327712 | tf_op jit(solution)/shard_map/all_to_all | solution.py:51
  175.5 0.3 copy.15
  175.9 0.9 fusion.5
  (53 shorter events, 2.1 us)
Async XLA Ops:
  6.5 158.3 %copy-start = (f32[4096]{0:T(1024)S(1)}, f32[4096]{0:T(1024)}, u32[]{:S(2)}) copy-start(f32[4096]{0:T(1024)} %param.13) | copy-start | bytes 49156
  6.5 15.7 %all-gather.5.cloned.1.call-start = ((), (), s32[]{:S(2)}) async-start(), calls=%async_computation.3 | async-start | bytes 3145728 | tf_op jit(solution)/shard_map/all_gather | solution.py:16
  7.3 117.2 %all-gather.3.cloned.1.call-start = ((), (), s32[]{:S(2)}) async-start(), calls=%async_computation.2 | async-start | bytes 5570560 | tf_op jit(solution)/shard_map/all_gather | solution.py:33
  143.7 21.0 %copy-start.3 = (s32[32]{0:T(128)S(1)}, s32[32]{0:T(128)}, u32[]{:S(2)}) copy-start(s32[32]{0:T(128)} %param.9) | copy-start | bytes 388
  144.5 15.1 %all-to-all-start = ((bf16[16,2,40,128]{3,1,2,0:T(2,128)(2,1)}), bf16[16,2,40,128]{3,1,2,0:T(2,128)(2,1)S(1)}, u32[]{:S(2)}, u32[]{:S(2)}) async-start(bf16[16,2,40,128]{3,1,2,0:T(2,128)(2,1)} %bitcast.9), calls=%async_computation | async-start | bytes 655360 | tf_op jit(solution)/shard_map/all_to_all | solution.py:49
  159.7 16.1 %copy-start.1 = (bf16[640,256]{1,0:T(8,128)(2,1)S(1)}, bf16[640,256]{1,0:T(8,128)(2,1)}, u32[]{:S(2)}) copy-start(bf16[640,256]{1,0:T(8,128)(2,1)} %param.8) | copy-start | bytes 983044
  159.7 16.1 %copy-start.2 = (f32[640]{0:T(1024)S(1)}, f32[640]{0:T(1024)}, u32[]{:S(2)}) copy-start(f32[640]{0:T(1024)} %param.12) | copy-start | bytes 7684
  161.2 14.3 %all-to-all-start.1 = ((bf16[16,2,40,128]{3,2,1,0:T(8,128)(2,1)}), bf16[16,2,40,128]{3,2,1,0:T(8,128)(2,1)S(1)}, u32[]{:S(2)}, u32[]{:S(2)}) async-start(bf16[16,2,40,128]{3,2,1,0:T(8,128)(2,1)} %broadcast_select_fusion.1), calls=%async_computation.1 | async-start | bytes 655360 | tf_op jit(solution)/shard_map/all_to_all | solution.py:51
Sparse Core Ops, SparseCore 0:
  8.9 13.2 all-gather.4
  24.9 99.5 all-gather.2

commit v2 on v1

v2 whole, which is shorter than its diff:
```python
import functools

import jax
import jax.numpy as jnp
from jax import lax
from jax.experimental import pallas as pl
from jax.experimental.pallas import tpu as pltpu
from jax.sharding import PartitionSpec as P

TILE = 128
PBLK = 64
KT_DEV = 2
MESH = pl.DeviceIdType.MESH


def one_hot(indices, length):
    return (indices[:, None] == jnp.arange(length, dtype=jnp.int32)[None, :]).astype(jnp.float32)


def ladder_kernel(
    ranks, pairs, owner, screen, amps, ints, out,
    gath, panel, lhs, acc,
    local_sem, send_sem, recv_sem, pair_send, pair_recv,
):
    length = ranks // 4
    me = lax.axis_index("vcol")
    core = lax.axis_index("pair")
    line, spot = me // 4, me % 4
    hi, lo = spot // 2, spot % 2
    turn = core % 2
    flip_lo, flip_hi = hi * 2 + 1 - lo, (1 - hi) * 2 + lo
    first = (1 - turn) * flip_lo + turn * flip_hi
    second = turn * flip_lo + (1 - turn) * flip_hi
    across = 3 - spot
    rows = gath.shape[1]
    blocks = rows // PBLK
    tiles = ints.shape[0]

    own_amps = pltpu.make_async_copy(amps, gath.at[me], local_sem.at[0])
    own_ints = pltpu.make_async_copy(ints, panel.at[pl.ds(core * tiles, tiles)], local_sem.at[1])
    own_amps.start()
    own_ints.start()

    has_up, has_down = line < length - 1, line > 0
    first_rank, second_rank = line * 4 + first, line * 4 + second
    barrier = pltpu.get_barrier_semaphore()

    def greet(target):
        pl.semaphore_signal(barrier, inc=1, device_id={"vcol": target}, device_id_type=MESH)

    greet(first_rank)
    greet(second_rank)
    for step in range(1, pairs):
        pl.semaphore_signal(
            barrier, inc=1, device_id={"pair": (core + step) % pairs}, device_id_type=MESH
        )

    @pl.when(has_up)
    def _():
        greet(me + 4)

    @pl.when(has_down)
    def _():
        greet(me - 4)

    pl.semaphore_wait(
        barrier, 1 + pairs + has_up.astype(jnp.int32) + has_down.astype(jnp.int32)
    )

    def shard(source, way, target):
        return pltpu.make_async_remote_copy(
            src_ref=gath.at[source], dst_ref=gath.at[source],
            send_sem=send_sem.at[way, source], recv_sem=recv_sem.at[source],
            device_id={"vcol": target}, device_id_type=MESH,
        )

    def panel_copy(step):
        return pltpu.make_async_remote_copy(
            src_ref=ints, dst_ref=panel.at[pl.ds(core * tiles, tiles)],
            send_sem=pair_send.at[step - 1], recv_sem=pair_recv.at[step - 1],
            device_id={"pair": (core + step) % pairs}, device_id_type=MESH,
        )

    def arrived(source):
        shard(source, 3, second_rank).wait_recv()

    def multiply(source):
        t0, t1 = owner[KT_DEV * source], owner[KT_DEV * source + 1]
        for slot, tile in enumerate((t0, t1)):
            columns = slice(slot * TILE, (slot + 1) * TILE)
            for block in range(blocks):
                part = slice(block * PBLK, (block + 1) * PBLK)
                value = gath[source, part, columns]
                for n in range(KT_DEV):
                    mark = screen[block, tile, KT_DEV * me + n].astype(jnp.float32)
                    lhs[n, part, columns] = value * jnp.full(value.shape, mark, jnp.float32).astype(
                        value.dtype
                    )
        right = jnp.concatenate([panel[t0], panel[t1]], axis=0)
        for n in range(KT_DEV):
            columns = slice(n * TILE, (n + 1) * TILE)
            acc[:, columns] += jnp.dot(
                lhs[n], right[:, columns], preferred_element_type=jnp.float32
            )

    def offset(e):
        return ((e + 1) // 2) * (1 - 2 * (e % 2))

    def inside(e):
        at = line + offset(e)
        return (at >= 0) & (at < length)

    own_amps.wait()

    @pl.when(has_up)
    def _():
        shard(me, 0, me + 4).start()

    @pl.when(has_down)
    def _():
        shard(me, 1, me - 4).start()

    shard(me, 2, first_rank).start()
    shard(me, 3, second_rank).start()
    for step in range(1, pairs):
        panel_copy(step).start()
    acc[...] = jnp.zeros_like(acc)
    own_ints.wait()
    for step in range(1, pairs):
        panel_copy(step).wait_recv()
    multiply(me)

    last = 2 * length - 1

    def on_column(e, _):
        source = (line + offset(e)) * 4 + spot

        @pl.when((e < last) & inside(e))
        def _():
            arrived(source)

            @pl.when((e % 2 == 1) & has_up)
            def _():
                shard(source, 0, me + 4).start()

            @pl.when((e % 2 == 0) & has_down)
            def _():
                shard(source, 1, me - 4).start()

            shard(source, 2, first_rank).start()
            shard(source, 3, second_rank).start()
            multiply(source)

        late = e - 2
        beside = (line + offset(late)) * 4 + first

        @pl.when((late >= 0) & inside(late))
        def _():
            arrived(beside)
            shard(beside, 3, second_rank).start()
            multiply(beside)

        return 0

    lax.fori_loop(1, last + 2, on_column, 0)

    def far_side(e, _):
        @pl.when((e < last) & inside(e))
        def _():
            source = (line + offset(e)) * 4 + second
            arrived(source)
            multiply(source)

        late = e - 2

        @pl.when((late >= 0) & inside(late))
        def _():
            source = (line + offset(late)) * 4 + across
            arrived(source)
            multiply(source)

        return 0

    lax.fori_loop(0, last + 2, far_side, 0)

    part = rows // ranks
    for i in range(ranks):
        for n in range(KT_DEV):
            out[i, n] = acc[i * part : (i + 1) * part, n * TILE : (n + 1) * TILE].astype(out.dtype)

    def drain(e, _):
        @pl.when(inside(e))
        def _():
            source = (line + offset(e)) * 4 + spot

            @pl.when(((e % 2 == 1) | (e == 0)) & has_up)
            def _():
                shard(source, 0, me + 4).wait_send()

            @pl.when((e % 2 == 0) & has_down)
            def _():
                shard(source, 1, me - 4).wait_send()

            shard(source, 2, first_rank).wait_send()
            shard(source, 3, second_rank).wait_send()
            shard((line + offset(e)) * 4 + first, 3, second_rank).wait_send()

        return 0

    lax.fori_loop(0, last, drain, 0)
    for step in range(1, pairs):
        panel_copy(step).wait_send()


def ladder(ranks, pairs, amplitudes, tile_owner, integrals, screening):
    rows, width = amplitudes.shape
    tiles = integrals.shape[0] // TILE
    vmem, smem = pl.BlockSpec(memory_space=pltpu.VMEM), pl.BlockSpec(memory_space=pltpu.SMEM)
    return pl.pallas_call(
        functools.partial(ladder_kernel, ranks, pairs),
        out_shape=jax.ShapeDtypeStruct((ranks, KT_DEV, rows // ranks, TILE), jnp.bfloat16),
        in_specs=[smem, smem, vmem, vmem],
        out_specs=vmem,
        scratch_shapes=[
            pltpu.VMEM((ranks, rows, width), jnp.bfloat16),
            pltpu.VMEM((tiles * pairs, TILE, width), jnp.bfloat16),
            pltpu.VMEM((KT_DEV, rows, width), jnp.bfloat16),
            pltpu.VMEM((rows, width), jnp.float32),
            pltpu.SemaphoreType.DMA((2,)),
            pltpu.SemaphoreType.DMA((4, ranks)),
            pltpu.SemaphoreType.DMA((ranks,)),
            pltpu.SemaphoreType.DMA((pairs - 1,)),
            pltpu.SemaphoreType.DMA((pairs - 1,)),
        ],
        compiler_params=pltpu.CompilerParams(
            collective_id=0, has_side_effects=True, vmem_limit_bytes=48 * 1024 * 1024
        ),
    )(tile_owner, screening, amplitudes, integrals.reshape(tiles, TILE, width))


def local(ranks, pairs, amplitudes, tile_owner, integrals, screening, occ_energy, virt_energy):
    pair_local = amplitudes.shape[0]
    tile_count = tile_owner.shape[0]
    width = KT_DEV * TILE
    column = lax.axis_index("vcol")
    owned_tiles = lax.dynamic_slice_in_dim(tile_owner, column * KT_DEV, KT_DEV, 0)
    rows = pair_local // ranks
    parts = ladder(ranks, pairs, amplitudes, tile_owner, integrals, screening)
    spread = lax.all_to_all(parts, "vcol", 0, 0, tiled=True).reshape(tile_count, rows, TILE)
    by_slot = jnp.take(spread, tile_owner, axis=0).reshape(ranks, KT_DEV, rows, TILE)
    back = lax.all_to_all(by_slot, "vcol", 0, 0, tiled=True)
    ladder_owned = back.transpose(0, 2, 1, 3).reshape(pair_local, width).astype(jnp.float32)
    virt_owned = jnp.dot(
        one_hot(owned_tiles, tile_count),
        virt_energy.reshape(tile_count, TILE),
        precision=lax.Precision.HIGHEST,
    ).reshape(width)
    residual = ladder_owned + (virt_owned[None, :] - occ_energy[:, None]) * amplitudes.astype(
        jnp.float32
    )
    return residual.astype(jnp.bfloat16)


def solution(mesh):
    return jax.shard_map(
        functools.partial(local, mesh.shape["vcol"], mesh.shape["pair"]),
        mesh=mesh,
        in_specs=(P("pair", "vcol"), P(), P("pair", "vcol"), P("pair", None, None), P("pair"), P()),
        out_specs=P("pair", "vcol"),
        check_vma=False,
    )
```

time: 185 us -> 92.4 us (0.50)
  waiting for transfers between devices: 131 us -> 22 us
  Pallas kernels: 0 us -> 54 us
  matrix products: 16.5 us -> 0.18 us
  between operations: 13.5 us -> 0.08 us
  other arithmetic: 6.53 us -> 2.25 us
  local copies, waits for them, and re-layouts: 8.64 us -> 5.02 us
    all_gather x2 -> x0, waiting for transfers between devices: 108 us -> none  [the longest x1 96.8 us: local(): piece_in = lax.all_gather(amplitudes, 'vcol', axis=1, tiled=True)]
    pallas_call x0 -> x1, Pallas kernels: none -> 54 us  [ladder(): pl.pallas_call(functools.partial(ladder_kernel, ranks, pairs), out_shape=...]
    dot_general x11 -> x0, matrix products: 16.3 us -> none  [the longest x10 15.1 us: one_block(): return jnp.dot(left_rows, masked, preferred_element_type=jnp.float32)]
    gather x2 -> x0, local copies, waits for them, and re-layouts: 4.27 us -> none  [the longest x1 3.67 us: local(): jnp.take(panel.reshape(tile_count, TILE, width), tile_owner, axis=0)]
    unnamed x8 -> x14, local copies, waits for them, and re-layouts: 0.02 us -> 4.24 us
    mul x30 -> x0, local copies, waits for them, and re-layouts: 2.08 us -> none  [one_block(): panel_slot.reshape(tiles_in, TILE, KT_DEV, TILE) * marks[:, None, :, None]]
  transfers between devices with their start and end apart: 4 -> 2, of which waited for: 4 -> 2; matrix products, arithmetic and copies ran while one was open for 5% -> 0% of each run, Pallas kernels for 0% -> 0%
where the time goes in v2:
time: 92.4 us; the launch traced here: 91.9 us
  Pallas kernels  54 us (58%)
  waiting for transfers between devices  22 us (24%)
  starting transfers between devices  8.37 us (9%)
  local copies, waits for them, and re-layouts  5.02 us (5%)
  other arithmetic  2.25 us (2%)
    pallas_call x1, Pallas kernels, ladder(): pl.pallas_call(functools.partial(ladder_kernel, ranks, pairs), out_shape=...  54 us
    all_to_all x1, waiting for transfers between devices, local(): lax.all_to_all(parts, 'vcol', 0, 0, tiled=True)  11.4 us
    all_to_all x1, waiting for transfers between devices, local(): back = lax.all_to_all(by_slot, 'vcol', 0, 0, tiled=True)  10.5 us
    all_to_all x1, starting transfers between devices, local(): lax.all_to_all(parts, 'vcol', 0, 0, tiled=True)  4.83 us
    unnamed x14, local copies, waits for them, and re-layouts  4.24 us
    all_to_all x1, starting transfers between devices, local(): back = lax.all_to_all(by_slot, 'vcol', 0, 0, tiled=True)  3.54 us
  transfers between devices with their start and end apart: 2, of which 2 were waited for; matrix products, arithmetic and copies ran while one was open for 0% of the time, Pallas kernels for 0%

profile of v2, /device:TPU:0, one launch (start us, length us, event | category | flops | bytes accessed | tf_op | source)
XLA Modules:
  0.0 91.9 jit_solution(2175160662722540216)
XLA Ops:
  0.0 0.0 copy-start
  0.0 0.0 copy-start.5
  0.0 0.7 copy-done.5
  0.7 0.0 copy-start.1
  0.7 1.0 %copy-done.1 = bf16[640,256]{1,0:T(8,128)(2,1)S(1)} copy-done((bf16[640,256]{1,0:T(8,128)(2,1)S(1)}, bf16[640,256]{1,0:T(8,128)(2,1)}, u32[]{:S(2)}) %copy-start.1) | copy-done | bytes 327704
  1.6 0.0 copy-start.3
  1.6 1.2 %copy-done.3 = bf16[2048,256]{1,0:T(8,128)(2,1)S(1)} copy-done((bf16[2048,256]{1,0:T(8,128)(2,1)S(1)}, bf16[2048,256]{1,0:T(8,128)(2,1)}, u32[]{:S(2)}) %copy-start.3) | copy-done | bytes 1048600
  2.9 0.0 copy-start.4
  2.9 0.9 copy-done.4
  3.8 54.0 %shard_map.64 = bf16[16,2,40,128]{3,2,1,0:T(8,128)(2,1)} custom-call(s32[32]{0:T(128)S(1)} %copy-done.5, s32[10,32,32]{2,1,0:T(8,128)S(1)} %copy-done.4, bf16[640,256]{1,0:T(8,128)(2,1)S(1)} %copy-done.1, bf16[16,128,256]{2,1,0:T(8,128)(2,1)S(1)} %bitcast.15), custom_call_target="tpu_custom_call" | custom-call | tf_op jit(solution)/shard_map/pallas_call | solution.py:219
  57.8 4.8 %all-to-all-start = ((bf16[16,2,40,128]{3,2,1,0:T(8,128)(2,1)}), bf16[16,2,40,128]{3,2,1,0:T(8,128)(2,1)S(1)}, u32[]{:S(2)}, u32[]{:S(2)}) async-start(bf16[16,2,40,128]{3,2,1,0:T(8,128)(2,1)} %shard_map.64), calls=%async_computation | async-start | bytes 655360 | tf_op jit(solution)/shard_map/all_to_all | solution.py:249
  62.7 0.1 broadcast_in_dim.17
  62.8 11.4 %all-to-all-done = bf16[16,2,40,128]{3,2,1,0:T(8,128)(2,1)S(1)} async-done(((bf16[16,2,40,128]{3,2,1,0:T(8,128)(2,1)}), bf16[16,2,40,128]{3,2,1,0:T(8,128)(2,1)S(1)}, u32[]{:S(2)}, u32[]{:S(2)}) %all-to-all-start) | async-done | bytes 327712 | tf_op jit(solution)/shard_map/all_to_all | solution.py:249
  74.2 0.6 gather_fusion
  74.8 1.1 %broadcast_select_fusion = bf16[16,2,40,128]{3,1,2,0:T(2,128)(2,1)} fusion(pred[16,2]{1,0:T(8,128)(4,1)S(1)} %broadcast_in_dim.17, bf16[16,2,40,128]{3,2,1,0:T(8,128)(2,1)S(1)} %bitcast.18), kind=kLoop, calls=%fused_computation.4 | loop fusion | flops 163840 | bytes 655392 | tf_op jit(solution)/shard_map/jit(_take)/select_n | solution.py:250
  75.9 3.5 %all-to-all-start.1 = ((bf16[16,2,40,128]{3,1,2,0:T(2,128)(2,1)}), bf16[16,2,40,128]{3,1,2,0:T(2,128)(2,1)S(1)}, u32[]{:S(2)}, u32[]{:S(2)}) async-start(bf16[16,2,40,128]{3,1,2,0:T(2,128)(2,1)} %broadcast_select_fusion), calls=%async_computation.1 | async-start | bytes 655360 | tf_op jit(solution)/shard_map/all_to_all | solution.py:251
  79.5 0.1 dynamic_slice.3
  79.6 0.0 copy-done
  79.6 0.2 convolution_bitcast_fusion
  79.8 0.0 copy-start.2
  79.8 10.5 %all-to-all-done.1 = bf16[16,2,40,128]{3,1,2,0:T(2,128)(2,1)S(1)} async-done(((bf16[16,2,40,128]{3,1,2,0:T(2,128)(2,1)}), bf16[16,2,40,128]{3,1,2,0:T(2,128)(2,1)S(1)}, u32[]{:S(2)}, u32[]{:S(2)}) %all-to-all-start.1) | async-done | bytes 327712 | tf_op jit(solution)/shard_map/all_to_all | solution.py:251
  90.3 0.0 copy-start.6
  90.3 0.2 convert_element_type.22
  90.5 0.0 copy-done.2
  90.6 0.4 copy-done.6
  91.0 0.9 fusion
  (3 shorter events, 0.0 us)
Async XLA Ops:
  0.0 79.6 %copy-start = (f32[4096]{0:T(1024)S(1)}, f32[4096]{0:T(1024)}, u32[]{:S(2)}) copy-start(f32[4096]{0:T(1024)} %param.11) | copy-start | bytes 49156
  0.0 0.7 copy-start.5
  0.7 1.0 %copy-start.1 = (bf16[640,256]{1,0:T(8,128)(2,1)S(1)}, bf16[640,256]{1,0:T(8,128)(2,1)}, u32[]{:S(2)}) copy-start(bf16[640,256]{1,0:T(8,128)(2,1)} %amps.1) | copy-start | bytes 983044
  1.6 1.2 %copy-start.3 = (bf16[2048,256]{1,0:T(8,128)(2,1)S(1)}, bf16[2048,256]{1,0:T(8,128)(2,1)}, u32[]{:S(2)}) copy-start(bf16[2048,256]{1,0:T(8,128)(2,1)} %param.8) | copy-start | bytes 3145732
  2.9 0.9 copy-start.4
  57.8 16.4 %all-to-all-start = ((bf16[16,2,40,128]{3,2,1,0:T(8,128)(2,1)}), bf16[16,2,40,128]{3,2,1,0:T(8,128)(2,1)S(1)}, u32[]{:S(2)}, u32[]{:S(2)}) async-start(bf16[16,2,40,128]{3,2,1,0:T(8,128)(2,1)} %shard_map.64), calls=%async_computation | async-start | bytes 655360 | tf_op jit(solution)/shard_map/all_to_all | solution.py:249
  75.9 14.4 %all-to-all-start.1 = ((bf16[16,2,40,128]{3,1,2,0:T(2,128)(2,1)}), bf16[16,2,40,128]{3,1,2,0:T(2,128)(2,1)S(1)}, u32[]{:S(2)}, u32[]{:S(2)}) async-start(bf16[16,2,40,128]{3,1,2,0:T(2,128)(2,1)} %broadcast_select_fusion), calls=%async_computation.1 | async-start | bytes 655360 | tf_op jit(solution)/shard_map/all_to_all | solution.py:251
  79.8 10.8 %copy-start.2 = (bf16[640,256]{1,0:T(8,128)(2,1)S(1)}, bf16[640,256]{1,0:T(8,128)(2,1)}, u32[]{:S(2)}) copy-start(bf16[640,256]{1,0:T(8,128)(2,1)} %amps.1) | copy-start | bytes 983044
  90.3 0.7 copy-start.6

commit v3 on v2

--- a/solution.py
+++ b/solution.py
@@ -19,8 +19,8 @@
 
 def ladder_kernel(
     ranks, pairs, owner, screen, amps, ints, out,
-    gath, panel, lhs, acc,
-    local_sem, send_sem, recv_sem, pair_send, pair_recv,
+    gath, panel, lhs, acc, parts, natural, slots, landed,
+    local_sem, send_sem, recv_sem, pair_send, pair_recv, out_send, out_recv, back_send, back_recv,
 ):
     length = ranks // 4
     me = lax.axis_index("vcol")
@@ -48,24 +48,17 @@
     def greet(target):
         pl.semaphore_signal(barrier, inc=1, device_id={"vcol": target}, device_id_type=MESH)
 
-    greet(first_rank)
-    greet(second_rank)
+    def greet_step(step, _):
+        greet((me + step) % ranks)
+        return 0
+
+    lax.fori_loop(1, ranks, greet_step, 0)
     for step in range(1, pairs):
         pl.semaphore_signal(
             barrier, inc=1, device_id={"pair": (core + step) % pairs}, device_id_type=MESH
         )
 
-    @pl.when(has_up)
-    def _():
-        greet(me + 4)
-
-    @pl.when(has_down)
-    def _():
-        greet(me - 4)
-
-    pl.semaphore_wait(
-        barrier, 1 + pairs + has_up.astype(jnp.int32) + has_down.astype(jnp.int32)
-    )
+    pl.semaphore_wait(barrier, ranks - 1 + pairs - 1)
 
     def shard(source, way, target):
         return pltpu.make_async_remote_copy(
@@ -186,7 +179,48 @@
     part = rows // ranks
     for i in range(ranks):
         for n in range(KT_DEV):
-            out[i, n] = acc[i * part : (i + 1) * part, n * TILE : (n + 1) * TILE].astype(out.dtype)
+            parts[i, n] = acc[i * part : (i + 1) * part, n * TILE : (n + 1) * TILE].astype(
+                parts.dtype
+            )
+
+    def out_copy(step):
+        target = (me + step) % ranks
+        return pltpu.make_async_remote_copy(
+            src_ref=parts.at[target], dst_ref=natural.at[pl.ds(KT_DEV * me, KT_DEV)],
+            send_sem=out_send.at[step - 1], recv_sem=out_recv.at[step - 1],
+            device_id={"vcol": target}, device_id_type=MESH,
+        )
+
+    def back_copy(step):
+        target = (me + step) % ranks
+        return pltpu.make_async_remote_copy(
+            src_ref=slots.at[pl.ds(KT_DEV * target, KT_DEV)], dst_ref=landed.at[me],
+            send_sem=back_send.at[step - 1], recv_sem=back_recv.at[step - 1],
+            device_id={"vcol": target}, device_id_type=MESH,
+        )
+
+    def each_peer(action):
+        def body(step, _):
+            action(step)
+            return 0
+
+        lax.fori_loop(1, ranks, body, 0)
+
+    own_out = pltpu.make_async_copy(
+        parts.at[me], natural.at[pl.ds(KT_DEV * me, KT_DEV)], local_sem.at[2]
+    )
+    own_back = pltpu.make_async_copy(
+        slots.at[pl.ds(KT_DEV * me, KT_DEV)], landed.at[me], local_sem.at[3]
+    )
+    each_peer(lambda step: out_copy(step).start())
+    own_out.start()
+    own_out.wait()
+    each_peer(lambda step: out_copy(step).wait_recv())
+    for slot in range(KT_DEV * ranks):
+        slots[slot] = natural[owner[slot]]
+    each_peer(lambda step: back_copy(step).start())
+    own_back.start()
+    own_back.wait()
 
     def drain(e, _):
         @pl.when(inside(e))
@@ -210,30 +244,44 @@
     lax.fori_loop(0, last, drain, 0)
     for step in range(1, pairs):
         panel_copy(step).wait_send()
+    each_peer(lambda step: out_copy(step).wait_send())
+    each_peer(lambda step: back_copy(step).wait_recv())
+    out[...] = landed[...]
+    each_peer(lambda step: back_copy(step).wait_send())
 
 
 def ladder(ranks, pairs, amplitudes, tile_owner, integrals, screening):
     rows, width = amplitudes.shape
     tiles = integrals.shape[0] // TILE
     vmem, smem = pl.BlockSpec(memory_space=pltpu.VMEM), pl.BlockSpec(memory_space=pltpu.SMEM)
+    hbm = pl.BlockSpec(memory_space=pl.ANY)
+    part = rows // ranks
     return pl.pallas_call(
         functools.partial(ladder_kernel, ranks, pairs),
         out_shape=jax.ShapeDtypeStruct((ranks, KT_DEV, rows // ranks, TILE), jnp.bfloat16),
-        in_specs=[smem, smem, vmem, vmem],
+        in_specs=[smem, smem, hbm, hbm],
         out_specs=vmem,
         scratch_shapes=[
             pltpu.VMEM((ranks, rows, width), jnp.bfloat16),
             pltpu.VMEM((tiles * pairs, TILE, width), jnp.bfloat16),
             pltpu.VMEM((KT_DEV, rows, width), jnp.bfloat16),
             pltpu.VMEM((rows, width), jnp.float32),
-            pltpu.SemaphoreType.DMA((2,)),
+            pltpu.VMEM((ranks, KT_DEV, part, TILE), jnp.bfloat16),
+            pltpu.VMEM((ranks * KT_DEV, part, TILE), jnp.bfloat16),
+            pltpu.VMEM((ranks * KT_DEV, part, TILE), jnp.bfloat16),
+            pltpu.VMEM((ranks, KT_DEV, part, TILE), jnp.bfloat16),
+            pltpu.SemaphoreType.DMA((4,)),
             pltpu.SemaphoreType.DMA((4, ranks)),
             pltpu.SemaphoreType.DMA((ranks,)),
             pltpu.SemaphoreType.DMA((pairs - 1,)),
             pltpu.SemaphoreType.DMA((pairs - 1,)),
+            pltpu.SemaphoreType.DMA((ranks - 1,)),
+            pltpu.SemaphoreType.DMA((ranks - 1,)),
+            pltpu.SemaphoreType.DMA((ranks - 1,)),
+            pltpu.SemaphoreType.DMA((ranks - 1,)),
         ],
         compiler_params=pltpu.CompilerParams(
-            collective_id=0, has_side_effects=True, vmem_limit_bytes=48 * 1024 * 1024
+            collective_id=0, has_side_effects=True, vmem_limit_bytes=62 * 1024 * 1024
         ),
     )(tile_owner, screening, amplitudes, integrals.reshape(tiles, TILE, width))
 
@@ -244,11 +292,7 @@
     width = KT_DEV * TILE
     column = lax.axis_index("vcol")
     owned_tiles = lax.dynamic_slice_in_dim(tile_owner, column * KT_DEV, KT_DEV, 0)
-    rows = pair_local // ranks
-    parts = ladder(ranks, pairs, amplitudes, tile_owner, integrals, screening)
-    spread = lax.all_to_all(parts, "vcol", 0, 0, tiled=True).reshape(tile_count, rows, TILE)
-    by_slot = jnp.take(spread, tile_owner, axis=0).reshape(ranks, KT_DEV, rows, TILE)
-    back = lax.all_to_all(by_slot, "vcol", 0, 0, tiled=True)
+    back = ladder(ranks, pairs, amplitudes, tile_owner, integrals, screening)
     ladder_owned = back.transpose(0, 2, 1, 3).reshape(pair_local, width).astype(jnp.float32)
     virt_owned = jnp.dot(
         one_hot(owned_tiles, tile_count),

time: 92.4 us -> 76.9 us (0.83)
  waiting for transfers between devices: 22 us -> 0 us
  Pallas kernels: 54 us -> 72.5 us
  starting transfers between devices: 8.37 us -> 0 us
  local copies, waits for them, and re-layouts: 5.02 us -> 1.57 us
    all_to_all x2 -> x0, waiting for transfers between devices: 22 us -> none  [the longest x1 11.4 us: local(): lax.all_to_all(parts, 'vcol', 0, 0, tiled=True)]
    pallas_call x1, Pallas kernels: 54 us -> 72.5 us  [ladder(): pl.pallas_call(functools.partial(ladder_kernel, ranks, pairs), out_shape=...]
    all_to_all x2 -> x0, starting transfers between devices: 8.37 us -> none  [the longest x1 4.83 us: local(): lax.all_to_all(parts, 'vcol', 0, 0, tiled=True)]
    unnamed x14 -> x8, local copies, waits for them, and re-layouts: 4.24 us -> 1.16 us
    select_n x2 -> x0, other arithmetic: 1.11 us -> none  [local(): jnp.take(spread, tile_owner, axis=0).reshape(ranks, KT_DEV, rows, TILE)]
  transfers between devices with their start and end apart: 2 -> 0, of which waited for: 2 -> 0; matrix products, arithmetic and copies ran while one was open for 0% -> 0% of each run, Pallas kernels for 0% -> 0%
where the time goes in v3:
time: 76.9 us; the launch traced here: 76.2 us
  Pallas kernels  72.5 us (94%)
  other arithmetic  1.92 us (2%)
  local copies, waits for them, and re-layouts  1.57 us (2%)
    pallas_call x1, Pallas kernels, ladder(): pl.pallas_call(functools.partial(ladder_kernel, ranks, pairs), out_shape=...  72.5 us

profile of v3, /device:TPU:0, one launch (start us, length us, event | category | flops | bytes accessed | tf_op | source)
XLA Modules:
  0.0 76.2 jit_solution(4869231791151971906)
XLA Ops:
  0.0 0.0 copy-start
  0.0 72.5 %shard_map.64 = bf16[16,2,40,128]{3,2,1,0:T(8,128)(2,1)} custom-call(s32[32]{0:T(128)} %owner.1, s32[10,32,32]{2,1,0:T(8,128)} %screen.1, bf16[640,256]{1,0:T(8,128)(2,1)} %amps.1, bf16[16,128,256]{2,1,0:T(8,128)(2,1)} %bitcast.15), custom_call_target="tpu_custom_call" | custom-call | tf_op jit(solution)/shard_map/pallas_call | solution.py:259
  72.5 1.0 %convert_bitcast_fusion = f32[16,40,2,128]{3,1,2,0:T(8,128)S(1)} fusion(bf16[16,2,40,128]{3,2,1,0:T(8,128)(2,1)} %shard_map.64), kind=kLoop, calls=%fused_computation.3 | loop fusion | flops 163840 | bytes 983040 | tf_op jit(solution)/shard_map/convert_element_type | solution.py:296
  73.6 0.0 copy-start.1
  73.6 0.3 copy.7
  73.9 0.0 copy-start.3
  73.9 0.6 copy-done.3
  74.6 0.1 dynamic_slice.3
  74.6 0.0 copy-done
  74.7 0.0 copy-start.2
  74.7 0.2 convolution_bitcast_fusion
  74.8 0.0 copy-done.1
  74.8 0.5 copy-done.2
  75.3 0.9 %fusion = bf16[640,256]{1,0:T(8,128)(2,1)} fusion(f32[80,8,2,128]{3,2,1,0:T(2,128)S(1)} %bitcast.14, bf16[640,256]{1,0:T(8,128)(2,1)S(1)} %copy-done.1, f32[640]{0:T(1024)S(1)} %copy-done.2, f32[256]{0:T(256)S(1)} %convolution_bitcast_fusion), kind=kLoop, calls=%fused_computation.2 | loop fusion | flops 819200 | bytes 1314304 | tf_op jit(solution)/shard_map/convert_element_type | solution.py:305
Async XLA Ops:
  0.0 74.6 %copy-start = (f32[4096]{0:T(1024)S(1)}, f32[4096]{0:T(1024)}, u32[]{:S(2)}) copy-start(f32[4096]{0:T(1024)} %param.11) | copy-start | bytes 49156
  73.6 1.3 %copy-start.1 = (bf16[640,256]{1,0:T(8,128)(2,1)S(1)}, bf16[640,256]{1,0:T(8,128)(2,1)}, u32[]{:S(2)}) copy-start(bf16[640,256]{1,0:T(8,128)(2,1)} %amps.1) | copy-start | bytes 983044
  73.9 0.7 copy-start.3
  74.7 0.7 copy-start.2

commit v4 on v3

--- a/solution.py
+++ b/solution.py
@@ -60,10 +60,15 @@
 
     pl.semaphore_wait(barrier, ranks - 1 + pairs - 1)
 
-    def shard(source, way, target):
+    cut = (blocks * 2 // 5) * PBLK
+    bands = ((0, cut), (cut, rows))
+
+    def shard(source, band, way, target):
+        low, high = bands[band]
+        place = gath.at[source, pl.ds(low, high - low)]
         return pltpu.make_async_remote_copy(
-            src_ref=gath.at[source], dst_ref=gath.at[source],
-            send_sem=send_sem.at[way, source], recv_sem=recv_sem.at[source],
+            src_ref=place, dst_ref=place,
+            send_sem=send_sem.at[band, way, source], recv_sem=recv_sem.at[band, source],
             device_id={"vcol": target}, device_id_type=MESH,
         )
 
@@ -74,14 +79,15 @@
             device_id={"pair": (core + step) % pairs}, device_id_type=MESH,
         )
 
-    def arrived(source):
-        shard(source, 3, second_rank).wait_recv()
-
-    def multiply(source):
+    def arrived(source, band):
+        shard(source, band, 3, second_rank).wait_recv()
+
+    def multiply(source, band):
+        low, high = bands[band]
         t0, t1 = owner[KT_DEV * source], owner[KT_DEV * source + 1]
         for slot, tile in enumerate((t0, t1)):
             columns = slice(slot * TILE, (slot + 1) * TILE)
-            for block in range(blocks):
+            for block in range(low // PBLK, high // PBLK):
                 part = slice(block * PBLK, (block + 1) * PBLK)
                 value = gath[source, part, columns]
                 for n in range(KT_DEV):
@@ -92,8 +98,8 @@
         right = jnp.concatenate([panel[t0], panel[t1]], axis=0)
         for n in range(KT_DEV):
             columns = slice(n * TILE, (n + 1) * TILE)
-            acc[:, columns] += jnp.dot(
-                lhs[n], right[:, columns], preferred_element_type=jnp.float32
+            acc[low:high, columns] += jnp.dot(
+                lhs[n, low:high], right[:, columns], preferred_element_type=jnp.float32
             )
 
     def offset(e):
@@ -105,23 +111,36 @@
 
     own_amps.wait()
 
-    @pl.when(has_up)
-    def _():
-        shard(me, 0, me + 4).start()
-
-    @pl.when(has_down)
-    def _():
-        shard(me, 1, me - 4).start()
-
-    shard(me, 2, first_rank).start()
-    shard(me, 3, second_rank).start()
+    def along_line(source, band, e, action):
+        @pl.when(((e % 2 == 1) | (e == 0)) & has_up)
+        def _():
+            action(shard(source, band, 0, me + 4))
+
+        @pl.when((e % 2 == 0) & has_down)
+        def _():
+            action(shard(source, band, 1, me - 4))
+
+    def start(copy):
+        copy.start()
+
+    def wait_send(copy):
+        copy.wait_send()
+
+    def forward(source, band, e):
+        along_line(source, band, e, start)
+        shard(source, band, 2, first_rank).start()
+        shard(source, band, 3, second_rank).start()
+
+    for band in (1, 0):
+        forward(me, band, jnp.int32(0))
     for step in range(1, pairs):
         panel_copy(step).start()
     acc[...] = jnp.zeros_like(acc)
     own_ints.wait()
     for step in range(1, pairs):
         panel_copy(step).wait_recv()
-    multiply(me)
+    for band in (1, 0):
+        multiply(me, band)
 
     last = 2 * length - 1
 
@@ -130,47 +149,56 @@
 
         @pl.when((e < last) & inside(e))
         def _():
-            arrived(source)
-
-            @pl.when((e % 2 == 1) & has_up)
-            def _():
-                shard(source, 0, me + 4).start()
-
-            @pl.when((e % 2 == 0) & has_down)
-            def _():
-                shard(source, 1, me - 4).start()
-
-            shard(source, 2, first_rank).start()
-            shard(source, 3, second_rank).start()
-            multiply(source)
+            for band in (1, 0):
+                arrived(source, band)
+                forward(source, band, e)
+            for band in (1, 0):
+                multiply(source, band)
 
         late = e - 2
         beside = (line + offset(late)) * 4 + first
 
-        @pl.when((late >= 0) & inside(late))
-        def _():
-            arrived(beside)
-            shard(beside, 3, second_rank).start()
-            multiply(beside)
+        @pl.when((late >= 0) & (late < last) & inside(late))
+        def _():
+            arrived(beside, 1)
+
+            @pl.when(late == 0)
+            def _():
+                shard(beside, 1, 3, second_rank).start()
+
+            arrived(beside, 0)
+            shard(beside, 0, 3, second_rank).start()
+            for band in (1, 0):
+                multiply(beside, band)
+
+        later = e - 4
+        corner = (line + offset(later)) * 4 + across
+
+        @pl.when((later >= 0) & inside(later))
+        def _():
+            arrived(corner, 1)
+            along_line(corner, 1, later, start)
+            multiply(corner, 1)
 
         return 0
 
-    lax.fori_loop(1, last + 2, on_column, 0)
+    lax.fori_loop(1, last + 4, on_column, 0)
 
     def far_side(e, _):
         @pl.when((e < last) & inside(e))
         def _():
             source = (line + offset(e)) * 4 + second
-            arrived(source)
-            multiply(source)
+            for band in (1, 0):
+                arrived(source, band)
+                multiply(source, band)
 
         late = e - 2
 
         @pl.when((late >= 0) & inside(late))
         def _():
             source = (line + offset(late)) * 4 + across
-            arrived(source)
-            multiply(source)
+            arrived(source, 0)
+            multiply(source, 0)
 
         return 0
 
@@ -225,22 +253,17 @@
     def drain(e, _):
         @pl.when(inside(e))
         def _():
-            source = (line + offset(e)) * 4 + spot
-
-            @pl.when(((e % 2 == 1) | (e == 0)) & has_up)
-            def _():
-                shard(source, 0, me + 4).wait_send()
-
-            @pl.when((e % 2 == 0) & has_down)
-            def _():
-                shard(source, 1, me - 4).wait_send()
-
-            shard(source, 2, first_rank).wait_send()
-            shard(source, 3, second_rank).wait_send()
-            shard((line + offset(e)) * 4 + first, 3, second_rank).wait_send()
+            level = (line + offset(e)) * 4
+            for band in (1, 0):
+                along_line(level + spot, band, e, wait_send)
+                shard(level + spot, band, 2, first_rank).wait_send()
+                shard(level + spot, band, 3, second_rank).wait_send()
+            shard(level + first, 0, 3, second_rank).wait_send()
+            along_line(level + across, 1, e, wait_send)
 
         return 0
 
+    shard(first_rank, 1, 3, second_rank).wait_send()
     lax.fori_loop(0, last, drain, 0)
     for step in range(1, pairs):
         panel_copy(step).wait_send()
@@ -271,8 +294,8 @@
             pltpu.VMEM((ranks * KT_DEV, part, TILE), jnp.bfloat16),
             pltpu.VMEM((ranks, KT_DEV, part, TILE), jnp.bfloat16),
             pltpu.SemaphoreType.DMA((4,)),
-            pltpu.SemaphoreType.DMA((4, ranks)),
-            pltpu.SemaphoreType.DMA((ranks,)),
+            pltpu.SemaphoreType.DMA((2, 4, ranks)),
+            pltpu.SemaphoreType.DMA((2, ranks)),
             pltpu.SemaphoreType.DMA((pairs - 1,)),
             pltpu.SemaphoreType.DMA((pairs - 1,)),
             pltpu.SemaphoreType.DMA((ranks - 1,)),

time: 76.9 us -> 78.3 us (1.018)
  Pallas kernels: 72.5 us -> 74.3 us
    pallas_call x1, Pallas kernels: 72.5 us -> 74.3 us  [ladder(): pl.pallas_call(functools.partial(ladder_kernel, ranks, pairs), out_shape=...]
where the time goes in v4:
time: 78.3 us; the launch traced here: 78 us
  Pallas kernels  74.3 us (95%)
  other arithmetic  1.92 us (2%)
  local copies, waits for them, and re-layouts  1.57 us (2%)
    pallas_call x1, Pallas kernels, ladder(): pl.pallas_call(functools.partial(ladder_kernel, ranks, pairs), out_shape=...  74.3 us

profile of v4, /device:TPU:0, one launch (start us, length us, event | category | flops | bytes accessed | tf_op | source)
XLA Modules:
  0.0 78.0 jit_solution(13571797778564808249)
XLA Ops:
  0.0 0.0 copy-start
  0.0 74.3 %shard_map.64 = bf16[16,2,40,128]{3,2,1,0:T(8,128)(2,1)} custom-call(s32[32]{0:T(128)} %owner.1, s32[10,32,32]{2,1,0:T(8,128)} %screen.1, bf16[640,256]{1,0:T(8,128)(2,1)} %amps.1, bf16[16,128,256]{2,1,0:T(8,128)(2,1)} %bitcast.15), custom_call_target="tpu_custom_call" | custom-call | tf_op jit(solution)/shard_map/pallas_call | solution.py:282
  74.3 1.0 %convert_bitcast_fusion = f32[16,40,2,128]{3,1,2,0:T(8,128)S(1)} fusion(bf16[16,2,40,128]{3,2,1,0:T(8,128)(2,1)} %shard_map.64), kind=kLoop, calls=%fused_computation.3 | loop fusion | flops 163840 | bytes 983040 | tf_op jit(solution)/shard_map/convert_element_type | solution.py:319
  75.4 0.0 copy-start.1
  75.4 0.3 copy.7
  75.7 0.0 copy-start.3
  75.7 0.6 copy-done.3
  76.4 0.1 dynamic_slice.3
  76.4 0.0 copy-done
  76.5 0.0 copy-start.2
  76.5 0.2 convolution_bitcast_fusion
  76.6 0.0 copy-done.1
  76.6 0.5 copy-done.2
  77.1 0.9 %fusion = bf16[640,256]{1,0:T(8,128)(2,1)} fusion(f32[80,8,2,128]{3,2,1,0:T(2,128)S(1)} %bitcast.14, bf16[640,256]{1,0:T(8,128)(2,1)S(1)} %copy-done.1, f32[640]{0:T(1024)S(1)} %copy-done.2, f32[256]{0:T(256)S(1)} %convolution_bitcast_fusion), kind=kLoop, calls=%fused_computation.2 | loop fusion | flops 819200 | bytes 1314304 | tf_op jit(solution)/shard_map/convert_element_type | solution.py:328
Async XLA Ops:
  0.0 76.5 %copy-start = (f32[4096]{0:T(1024)S(1)}, f32[4096]{0:T(1024)}, u32[]{:S(2)}) copy-start(f32[4096]{0:T(1024)} %param.11) | copy-start | bytes 49156
  75.4 1.3 %copy-start.1 = (bf16[640,256]{1,0:T(8,128)(2,1)S(1)}, bf16[640,256]{1,0:T(8,128)(2,1)}, u32[]{:S(2)}) copy-start(bf16[640,256]{1,0:T(8,128)(2,1)} %amps.1) | copy-start | bytes 983044
  75.7 0.7 copy-start.3
  76.5 0.7 copy-start.2

commit v5 on v4

--- a/solution.py
+++ b/solution.py
@@ -60,7 +60,7 @@
 
     pl.semaphore_wait(barrier, ranks - 1 + pairs - 1)
 
-    cut = (blocks * 2 // 5) * PBLK
+    cut = (blocks * 3 // 5) * PBLK
     bands = ((0, cut), (cut, rows))
 
     def shard(source, band, way, target):

time: 78.3 us -> 72 us (0.920)
  Pallas kernels: 74.3 us -> 67.8 us
    pallas_call x1, Pallas kernels: 74.3 us -> 67.8 us  [ladder(): pl.pallas_call(functools.partial(ladder_kernel, ranks, pairs), out_shape=...]
where the time goes in v5:
time: 72 us; the launch traced here: 71.5 us
  Pallas kernels  67.8 us (94%)
  other arithmetic  1.92 us (3%)
  local copies, waits for them, and re-layouts  1.57 us (2%)
    pallas_call x1, Pallas kernels, ladder(): pl.pallas_call(functools.partial(ladder_kernel, ranks, pairs), out_shape=...  67.8 us

profile of v5, /device:TPU:0, one launch (start us, length us, event | category | flops | bytes accessed | tf_op | source)
XLA Modules:
  0.0 71.5 jit_solution(14177432085863900104)
XLA Ops:
  0.0 0.0 copy-start
  0.0 67.8 %shard_map.64 = bf16[16,2,40,128]{3,2,1,0:T(8,128)(2,1)} custom-call(s32[32]{0:T(128)} %owner.1, s32[10,32,32]{2,1,0:T(8,128)} %screen.1, bf16[640,256]{1,0:T(8,128)(2,1)} %amps.1, bf16[16,128,256]{2,1,0:T(8,128)(2,1)} %bitcast.15), custom_call_target="tpu_custom_call" | custom-call | tf_op jit(solution)/shard_map/pallas_call | solution.py:282
  67.8 1.0 %convert_bitcast_fusion = f32[16,40,2,128]{3,1,2,0:T(8,128)S(1)} fusion(bf16[16,2,40,128]{3,2,1,0:T(8,128)(2,1)} %shard_map.64), kind=kLoop, calls=%fused_computation.3 | loop fusion | flops 163840 | bytes 983040 | tf_op jit(solution)/shard_map/convert_element_type | solution.py:319
  68.8 0.0 copy-start.1
  68.8 0.3 copy.7
  69.2 0.0 copy-start.3
  69.2 0.6 copy-done.3
  69.8 0.1 dynamic_slice.3
  69.9 0.0 copy-done
  69.9 0.0 copy-start.2
  69.9 0.2 convolution_bitcast_fusion
  70.1 0.0 copy-done.1
  70.1 0.5 copy-done.2
  70.6 0.9 %fusion = bf16[640,256]{1,0:T(8,128)(2,1)} fusion(f32[80,8,2,128]{3,2,1,0:T(2,128)S(1)} %bitcast.14, bf16[640,256]{1,0:T(8,128)(2,1)S(1)} %copy-done.1, f32[640]{0:T(1024)S(1)} %copy-done.2, f32[256]{0:T(256)S(1)} %convolution_bitcast_fusion), kind=kLoop, calls=%fused_computation.2 | loop fusion | flops 819200 | bytes 1314304 | tf_op jit(solution)/shard_map/convert_element_type | solution.py:328
Async XLA Ops:
  0.0 69.9 %copy-start = (f32[4096]{0:T(1024)S(1)}, f32[4096]{0:T(1024)}, u32[]{:S(2)}) copy-start(f32[4096]{0:T(1024)} %param.11) | copy-start | bytes 49156
  68.8 1.3 %copy-start.1 = (bf16[640,256]{1,0:T(8,128)(2,1)S(1)}, bf16[640,256]{1,0:T(8,128)(2,1)}, u32[]{:S(2)}) copy-start(bf16[640,256]{1,0:T(8,128)(2,1)} %amps.1) | copy-start | bytes 983044
  69.2 0.7 copy-start.3
  69.9 0.7 copy-start.2

commit v6 on v5

--- a/solution.py
+++ b/solution.py
@@ -269,7 +269,9 @@
         panel_copy(step).wait_send()
     each_peer(lambda step: out_copy(step).wait_send())
     each_peer(lambda step: back_copy(step).wait_recv())
-    out[...] = landed[...]
+    for i in range(ranks):
+        for n in range(KT_DEV):
+            out[i * part : (i + 1) * part, n * TILE : (n + 1) * TILE] = landed[i, n].astype(out.dtype)
     each_peer(lambda step: back_copy(step).wait_send())
 
 
@@ -281,7 +283,7 @@
     part = rows // ranks
     return pl.pallas_call(
         functools.partial(ladder_kernel, ranks, pairs),
-        out_shape=jax.ShapeDtypeStruct((ranks, KT_DEV, rows // ranks, TILE), jnp.bfloat16),
+        out_shape=jax.ShapeDtypeStruct((rows, width), jnp.float32),
         in_specs=[smem, smem, hbm, hbm],
         out_specs=vmem,
         scratch_shapes=[
@@ -315,8 +317,7 @@
     width = KT_DEV * TILE
     column = lax.axis_index("vcol")
     owned_tiles = lax.dynamic_slice_in_dim(tile_owner, column * KT_DEV, KT_DEV, 0)
-    back = ladder(ranks, pairs, amplitudes, tile_owner, integrals, screening)
-    ladder_owned = back.transpose(0, 2, 1, 3).reshape(pair_local, width).astype(jnp.float32)
+    ladder_owned = ladder(ranks, pairs, amplitudes, tile_owner, integrals, screening)
     virt_owned = jnp.dot(
         one_hot(owned_tiles, tile_count),
         virt_energy.reshape(tile_count, TILE),

time: 72 us -> 71.4 us (level)
  local copies, waits for them, and re-layouts: 1.57 us -> 0.75 us
    convert_element_type x1, other arithmetic: 0.91 us -> 1.99 us  [local(): return residual.astype(jnp.bfloat16)]
    convert_element_type x1 -> x0, other arithmetic: 1.02 us -> none  [local(): back.transpose(0, 2, 1, 3).reshape(pair_local, width).astype(jnp.float32)]
where the time goes in v6:
time: 71.4 us; the launch traced here: 70.9 us
  Pallas kernels  67.9 us (95%)
  other arithmetic  1.99 us (3%)
  local copies, waits for them, and re-layouts  0.75 us (1%)
    pallas_call x1, Pallas kernels, ladder(): pl.pallas_call(functools.partial(ladder_kernel, ranks, pairs), out_shape=...  67.9 us
    convert_element_type x1, other arithmetic, local(): return residual.astype(jnp.bfloat16)  1.99 us

profile of v6, /device:TPU:0, one launch (start us, length us, event | category | flops | bytes accessed | tf_op | source)
XLA Modules:
  0.0 70.9 jit_solution(8663564225694767419)
XLA Ops:
  0.0 0.0 copy-start
  0.0 0.0 copy-start.3
  0.0 0.7 copy-done.3
  0.7 0.1 dynamic_slice.3
  0.7 0.0 copy-done
  0.7 0.2 convolution_bitcast_fusion
  0.9 0.0 copy-start.1
  0.9 0.0 copy-start.2
  0.9 67.9 %shard_map.64 = f32[640,256]{1,0:T(8,128)} custom-call(s32[32]{0:T(128)} %owner.1, s32[10,32,32]{2,1,0:T(8,128)} %screen.1, bf16[640,256]{1,0:T(8,128)(2,1)} %amps.1, bf16[16,128,256]{2,1,0:T(8,128)(2,1)} %bitcast.6), custom_call_target="tpu_custom_call" | custom-call | tf_op jit(solution)/shard_map/pallas_call | solution.py:284
  68.9 0.0 copy-done.1
  68.9 0.0 copy-done.2
  68.9 2.0 %add_convert_fusion = bf16[640,256]{1,0:T(8,128)(2,1)} fusion(f32[640,256]{1,0:T(8,128)} %shard_map.64, bf16[640,256]{1,0:T(8,128)(2,1)S(1)} %copy-done.1, f32[640]{0:T(1024)S(1)} %copy-done.2, f32[256]{0:T(256)S(1)} %convolution_bitcast_fusion), kind=kLoop, calls=%fused_computation.1 | loop fusion | flops 819200 | bytes 1314304 | tf_op jit(solution)/shard_map/convert_element_type | solution.py:329
Async XLA Ops:
  0.0 0.7 %copy-start = (f32[4096]{0:T(1024)S(1)}, f32[4096]{0:T(1024)}, u32[]{:S(2)}) copy-start(f32[4096]{0:T(1024)} %param.11) | copy-start | bytes 49156
  0.0 0.7 copy-start.3
  0.9 67.9 %copy-start.1 = (bf16[640,256]{1,0:T(8,128)(2,1)S(1)}, bf16[640,256]{1,0:T(8,128)(2,1)}, u32[]{:S(2)}) copy-start(bf16[640,256]{1,0:T(8,128)(2,1)} %amps.1) | copy-start | bytes 983044
  0.9 67.9 %copy-start.2 = (f32[640]{0:T(1024)S(1)}, f32[640]{0:T(1024)}, u32[]{:S(2)}) copy-start(f32[640]{0:T(1024)} %param.10) | copy-start | bytes 7684
